TPU v7x, 32 devices: a whole 2x2x4 slice. The times are simulated.
32 devices in a mesh: groups: 2 (over y), fsdp: 4 (over z), dp: 4 (over x, core).
Axes of the slice: x: 2, y: 2, z: 4, core: 2. Of those that a mesh axis runs over, the one named last changes fastest.
Arguments:
- hidden_in: bfloat16 [4096, 8192], P(('groups', 'dp'), 'fsdp'), parts along dimension 0, may hold values from -6 to 6
- cotangent: bfloat16 [4096, 9216], P(('groups', 'dp'), 'fsdp'), parts along dimension 0, may hold values from -6 to 6
- base_codes: bfloat16 [8192, 9216], P('fsdp', 'dp'), may hold values from -1 to 1
- base_scales: bfloat16 [8192, 144], P('fsdp', 'dp'), may hold values from 0.0079956055 to 0.039794922
- factor_a: bfloat16 [32, 131072], P('groups', 'fsdp'), parts along dimension 0, may hold values from -0.0625 to 0.0625
- factor_b: bfloat16 [32, 73728], P('groups', 'fsdp'), parts along dimension 0, may hold values from -0.0625 to 0.0625
- task_state: bfloat16 [32, 512], P('groups', 'dp'), parts along dimension 0, may hold values from -0.1796875 to 0.1796875
- head_a: bfloat16 [512, 131072], P('dp', 'fsdp'), may hold values from -0.0004196167 to 0.0004196167
- head_b: bfloat16 [512, 73728], P('dp', 'fsdp'), may hold values from -0.0004196167 to 0.0004196167
- task_ids: int32 [8], P(('groups', 'dp')), parts along dimension 0, may hold values from 0 to 15
- valid_counts: int32 [8], P(('groups', 'dp')), parts along dimension 0, may hold values from 64 to 384, as said below
- owners: int32 [32], P('groups'), parts along dimension 0, may hold values from 0 to 3, as said below
Outputs:
- input_gradient: bfloat16 [4096, 8192], P(('groups', 'dp'), 'fsdp'), parts along dimension 0
- grad_head_a: float32 [1024, 131072], P(('groups', 'dp'), 'fsdp'), parts along dimension 0
- grad_head_b: float32 [1024, 73728], P(('groups', 'dp'), 'fsdp'), parts along dimension 0
- grad_state: float32 [32, 512], P(('groups', 'fsdp'), 'dp'), parts along dimension 0
There are 2 independent parts, one for each index of `groups`. A program takes and returns all parts, laid end to end along the dimension named above; an argument that names none is the same for every part. Nothing has to cross between parts.
Inputs may be any that keep to these rules, and one draw needn't show every extreme that they name: `valid_counts`: every sequence has at most 384 valid tokens, and some sequence has exactly 384. `owners`: no owner has more than 4 tasks, and some owner has exactly 4.
All inputs are finite; a program needn't handle non-finite values.
Results may differ from a plain program's by a relative error of at most 0.017.
Values may be sent and summed in bfloat16 or wider, within the bound.
No kernel may reach another device: no remote copies, remote signals or barrier semaphores. Data moves between devices by JAX's collectives and lax.ppermute only.
A program may use at most 320 MiB of HBM per device.

v0:
```python
import jax
import jax.numpy as jnp
from jax import lax
from jax.sharding import PartitionSpec as P

HEADS = 64
KV_HEADS = 8
HEAD_DIM = 128
QBLOCK = 64
SLOTS = 4
adapter_scale = 2.0


def shards(
    hidden_in,
    cotangent,
    base_codes,
    base_scales,
    factor_a,
    factor_b,
    task_state,
    head_a,
    head_b,
    task_ids,
    valid_counts,
    owners,
):
    highest = lax.Precision.HIGHEST
    seq_len, width_part = hidden_in.shape
    tasks_all, factor_cols = factor_a.shape
    rank_double = factor_cols // width_part
    rank_half = rank_double // 2
    joined_part = cotangent.shape[1]
    positions = lax.broadcasted_iota(jnp.int32, (seq_len, 1), 0)
    row_keep = (positions < valid_counts[0]).astype(jnp.bfloat16)
    masked = cotangent * row_keep
    picked = (lax.broadcasted_iota(jnp.int32, (1, tasks_all), 1) == task_ids[0]).astype(
        jnp.bfloat16
    )
    chosen_a = (
        jnp.dot(picked, factor_a, preferred_element_type=jnp.float32)
        .astype(jnp.bfloat16)
        .reshape(width_part, rank_double)
    )
    chosen_b = (
        jnp.dot(picked, factor_b, preferred_element_type=jnp.float32)
        .astype(jnp.bfloat16)
        .reshape(joined_part, rank_half)
    )
    group_cols = (HEADS // KV_HEADS + 1) * HEAD_DIM
    columns = lax.axis_index("fsdp") * joined_part + lax.broadcasted_iota(
        jnp.int32, (joined_part, 1), 0
    )
    value_column_start = columns % group_cols >= HEADS // KV_HEADS * HEAD_DIM
    empty_b = jnp.zeros_like(chosen_b)
    joined_b = jnp.concatenate(
        [
            jnp.where(value_column_start, empty_b, chosen_b),
            jnp.where(value_column_start, chosen_b, empty_b),
        ],
        axis=1,
    )
    inner_part = jnp.dot(hidden_in, chosen_a, preferred_element_type=jnp.float32)
    outer_part = jnp.dot(masked, joined_b, preferred_element_type=jnp.float32)
    lowrank_in, lowrank_out = (
        lax.psum(inner_part.astype(jnp.bfloat16), "fsdp").astype(jnp.float32),
        lax.psum(outer_part.astype(jnp.bfloat16), "fsdp").astype(jnp.float32),
    )
    lowrank_low = lowrank_in.astype(jnp.bfloat16)
    reduced_rank_gradient = lowrank_out.astype(jnp.bfloat16)
    codes_all, scales_all = (
        lax.all_gather(base_codes, "dp", axis=1, tiled=True),
        lax.all_gather(base_scales, "dp", axis=1, tiled=True),
    )
    block_count = scales_all.shape[1]
    weight = (
        (
            codes_all.astype(jnp.float32).reshape(width_part, block_count, QBLOCK)
            * scales_all.astype(jnp.float32)[:, :, None]
        )
        .reshape(width_part, block_count * QBLOCK)
        .astype(jnp.bfloat16)
    )
    merged_rows = lax.dot_general(
        lax.all_gather(masked, "fsdp", axis=1, tiled=True),
        weight,
        (((1,), (1,)), ((), ())),
        preferred_element_type=jnp.float32,
    )
    adapter_contribution = lax.dot_general(
        reduced_rank_gradient,
        chosen_a,
        (((1,), (1,)), ((), ())),
        preferred_element_type=jnp.float32,
    )
    input_gradient = (merged_rows + adapter_scale * adapter_contribution).astype(jnp.bfloat16)
    down_gradient = adapter_scale * lax.dot_general(
        hidden_in,
        reduced_rank_gradient,
        (((0,), (0,)), ((), ())),
        preferred_element_type=jnp.float32,
    )
    mixed_products = lax.dot_general(
        masked, lowrank_low, (((0,), (0,)), ((), ())), preferred_element_type=jnp.float32
    )
    up_gradient = adapter_scale * jnp.where(
        value_column_start, mixed_products[:, rank_half:], mixed_products[:, :rank_half]
    )
    task_column = picked.astype(jnp.float32).reshape(tasks_all, 1)
    task_down = task_column * down_gradient.reshape(1, -1)
    task_up = task_column * up_gradient.reshape(1, -1)
    sum_down, sum_up = (
        lax.psum(task_down.astype(jnp.bfloat16), "dp").astype(jnp.float32),
        lax.psum(task_up.astype(jnp.bfloat16), "dp").astype(jnp.float32),
    )
    state_wide = task_state.astype(jnp.float32)
    grad_head_a = lax.dot_general(state_wide, sum_down, (((0,), (0,)), ((), ())), precision=highest)
    grad_head_b = lax.dot_general(state_wide, sum_up, (((0,), (0,)), ((), ())), precision=highest)
    state_part = lax.dot_general(
        sum_down, head_a.astype(jnp.float32), (((1,), (1,)), ((), ())), precision=highest
    )
    state_part = state_part + lax.dot_general(
        sum_up, head_b.astype(jnp.float32), (((1,), (1,)), ((), ())), precision=highest
    )
    task_rows = lax.broadcasted_iota(jnp.int32, (tasks_all, tasks_all), 0)
    task_other = lax.broadcasted_iota(jnp.int32, (tasks_all, tasks_all), 1)
    same_owner = owners[:, None] == owners[None, :]
    slot_index = jnp.sum((same_owner & (task_other < task_rows)).astype(jnp.int32), axis=1)
    target = owners * SLOTS + slot_index
    rows_all = lax.axis_size("fsdp") * SLOTS
    selector = (
        lax.broadcasted_iota(jnp.int32, (rows_all, tasks_all), 0) == target[None, :]
    ).astype(jnp.float32)
    owner_terms = jnp.dot(selector, state_part, precision=highest)
    grad_state = lax.psum_scatter(
        owner_terms.astype(jnp.bfloat16), "fsdp", scatter_dimension=0, tiled=True
    ).astype(jnp.float32)
    return (input_gradient, grad_head_a, grad_head_b, grad_state)


def solution(mesh):
    placed = (
        P(("groups", "dp"), "fsdp"),
        P(("groups", "dp"), "fsdp"),
        P("fsdp", "dp"),
        P("fsdp", "dp"),
        P("groups", "fsdp"),
        P("groups", "fsdp"),
        P("groups", "dp"),
        P("dp", "fsdp"),
        P("dp", "fsdp"),
        P(("groups", "dp")),
        P(("groups", "dp")),
        P("groups"),
    )
    return jax.shard_map(
        shards,
        mesh=mesh,
        in_specs=placed,
        out_specs=(
            P(("groups", "dp"), "fsdp"),
            P(("groups", "dp"), "fsdp"),
            P(("groups", "dp"), "fsdp"),
            P(("groups", "fsdp"), "dp"),
        ),
        check_vma=False,
    )
```

profile of v0, /device:TPU:0, one launch (start us, length us, event | category | flops | bytes accessed | tf_op | source)
XLA Modules:
  0.0 524.0 jit_solution(353779576208548617)
XLA Ops:
  7.2 0.0 copy-start
  7.2 0.0 all-reduce.5.cloned.1.call-start
  8.7 1.3 fusion.16
  10.0 0.7 reshape.72
  10.7 0.2 copy.34
  10.9 1.5 fusion.14
  12.4 0.4 reshape.73
  12.8 3.3 broadcast_multiply_fusion
  16.1 0.0 copy-done
  16.1 0.6 fusion.2
  16.8 2.4 convolution_convert_fusion.1
  19.2 20.8 %all-reduce.2 = (bf16[512,16]{0,1:T(8,128)(2,1)S(1)}, bf16[512,16]{0,1:T(8,128)(2,1)S(1)}) all-reduce(bf16[512,16]{0,1:T(8,128)(2,1)S(1)} %convolution_convert_fusion.1, bf16[512,16]{0,1:T(8,128)(2,1)S(1)} %fusion.2), channel_id=1, replica_groups=mesh['groups'=2,'fsdp'=4,'dp'=4] {'fsdp'}, use_global_device_ids=true, to_apply=%region_0.1 | all-reduce | flops 16384 | bytes 65536 | tf_op jit(solution)/shard_map/psum | solution.py:67
  40.0 0.4 fusion.1
  40.4 0.3 copy.36
  40.7 0.3 mul.88
  41.0 2.1 fusion.23
  43.2 0.4 copy.37
  43.5 0.6 mul.94
  44.1 1.2 multiply_convert_fusion
  45.2 0.9 multiply_convert_fusion.1
  46.2 0.0 all-reduce.5.cloned.1.call-update
  46.2 0.0 all-gather.6.cloned.1.call-start
  46.3 12.7 %copy.33 = bf16[2048,2304]{0,1:T(8,128)(2,1)} copy(bf16[2048,2304]{1,0:T(8,128)(2,1)} %param.14) | data formatting | bytes 18874368 | tf_op args[2]
  58.9 0.0 copy-start.5
  58.9 0.0 all-gather.6.cloned.1.call-update
  59.0 0.0 copy-start.8
  59.0 0.0 copy-start.7
  59.0 0.0 copy-start.6
  59.0 0.0 all-gather.4.cloned.1.call-start
  59.1 0.7 all-gather.4.cloned.1.call-update
  59.7 0.1 copy-done.5
  59.9 9.7 %all-gather = bf16[4,36,2048]{2,1,0:T(8,128)(2,1)S(1)} all-gather(bf16[1,36,2048]{2,1,0:T(8,128)(2,1)S(1)} %bitcast.56), channel_id=1, replica_groups=mesh['groups'=2,'fsdp'=4,'dp'=4] {'dp'}, dimensions={0}, use_global_device_ids=true | all-gather | bytes 737280 | tf_op jit(solution)/shard_map/all_gather | solution.py:73
  69.6 1.1 reshape.76
  70.7 0.0 copy-done.8
  70.7 0.6 dynamic-slice
  71.9 0.0 copy-done.7
  72.0 0.2 convert_reduce_fusion
  72.1 20.1 %all-reduce.5.cloned.1.call-done = (bf16[16,32768]{1,0:T(8,128)(2,1)}, bf16[16,18432]{1,0:T(8,128)(2,1)}) async-done(((bf16[16,32768]{1,0:T(8,128)(2,1)}, bf16[16,18432]{1,0:T(8,128)(2,1)}), (bf16[16,32768]{1,0:T(8,128)(2,1)}, bf16[16,18432]{1,0:T(8,128)(2,1)})) %all-reduce.5.cloned.1.call-update) | async-done | bytes 1638416 | tf_op jit(solution)/shard_map/psum | solution.py:113
  92.2 0.0 copy-done.6
  92.2 11.6 %convolution_bitcast_fusion = f32[128,32768]{0,1:T(8,128)} fusion(bf16[16,32768]{1,0:T(8,128)(2,1)} %get-tuple-element.20, bf16[16,128]{1,0:T(8,128)(2,1)S(1)} %copy-done.6), kind=kOutput, calls=%fused_computation.2 | convolution fusion | flops 134217728 | bytes 17829888 | tf_op jit(solution)/shard_map/dot_general | solution.py:117
  103.8 0.0 copy-start.4
  103.8 19.4 %copy.38 = f32[128,32768]{1,0:T(8,128)} copy(f32[128,32768]{0,1:T(8,128)} %convolution_bitcast_fusion) | data formatting | bytes 33554432
  123.2 0.0 copy-done.4
  123.2 4.6 convolution_bitcast_fusion.1
  127.8 0.0 copy-start.2
  127.8 9.7 %copy.39 = f32[128,18432]{1,0:T(8,128)} copy(f32[128,18432]{0,1:T(8,128)} %convolution_bitcast_fusion.1) | data formatting | bytes 18874368
  137.4 0.0 copy-done.2
  137.4 5.6 %fusion.22 = f32[16,128]{1,0:T(8,128)S(1)} fusion(bf16[16,32768]{1,0:T(8,128)(2,1)S(1)} %copy-done.2, bf16[128,32768]{1,0:T(8,128)(2,1)} %param.19), kind=kOutput, calls=%fused_computation.47 | convolution fusion | flops 134217728 | bytes 9445376 | tf_op jit(solution)/shard_map/dot_general | solution.py:119
  143.1 0.0 copy-start.3
  143.1 3.8 convolution_add_fusion
  146.9 0.1 convolution_convert_fusion.2
  147.0 11.6 %all-reduce = bf16[16,128]{1,0:T(8,128)(2,1)S(1)} all-reduce(bf16[16,128]{1,0:T(8,128)(2,1)S(1)} %convolution_convert_fusion.2), channel_id=2, replica_groups=mesh['groups'=2,'fsdp'=4,'dp'=4] {'fsdp'}, use_global_device_ids=true, to_apply=%region_5.6.clone | all-reduce | flops 2048 | bytes 8192
  158.6 0.6 dynamic-slice_convert_fusion
  159.2 161.9 %all-gather.6.cloned.1.call-done = bf16[2048,9216]{0,1:T(8,128)(2,1)} async-done(((bf16[2048,2304]{0,1:T(8,128)(2,1)}), bf16[2048,9216]{0,1:T(8,128)(2,1)}) %all-gather.6.cloned.1.call-update) | async-done | bytes 37748752 | tf_op jit(solution)/shard_map/all_gather | solution.py:72
  321.2 0.0 copy-done.3
  321.2 26.4 %fusion = bf16[2048,9216]{0,1:T(8,128)(2,1)} fusion(bf16[2048,9216]{0,1:T(8,128)(2,1)} %all-gather.6.cloned.1.call-done, f32[2048,144]{0,1:T(8,128)S(1)} %bitcast.53), kind=kLoop, calls=%fused_computation.1 | loop fusion | flops 56623104 | bytes 76677120 | tf_op jit(solution)/shard_map/convert_element_type | solution.py:82
  347.6 142.0 %all-gather.4.cloned.1.call-done = bf16[512,9216]{1,0:T(8,128)(2,1)} async-done(((bf16[512,2304]{1,0:T(8,128)(2,1)}), bf16[512,9216]{1,0:T(8,128)(2,1)}) %all-gather.4.cloned.1.call-update) | async-done | bytes 9437200 | tf_op jit(solution)/shard_map/all_gather | solution.py:85
  489.6 0.0 copy-start.1
  489.6 25.8 %fusion.21 = f32[512,2048]{1,0:T(8,128)S(1)} fusion(bf16[512,9216]{1,0:T(8,128)(2,1)} %all-gather.4.cloned.1.call-done, bf16[2048,9216]{0,1:T(8,128)(2,1)} %fusion), kind=kOutput, calls=%fused_computation.46 | convolution fusion | flops 19327352832 | bytes 51380224 | tf_op jit(solution)/shard_map/dot_general | solution.py:84
  515.4 2.1 add_convert_fusion
  517.5 0.0 copy-done.1
  (8 shorter events, 0.1 us)
Async XLA Ops:
  7.2 9.0 %copy-start = (bf16[512,2048]{1,0:T(8,128)(2,1)S(1)}, bf16[512,2048]{1,0:T(8,128)(2,1)}, u32[]{:S(2)}) copy-start(bf16[512,2048]{1,0:T(8,128)(2,1)} %param.12) | copy-start | bytes 6291460
  7.2 85.0 %all-reduce.5.cloned.1.call-start = ((), (), s32[]{:S(2)}) async-start(), calls=%async_computation.2 | async-start | bytes 3276800 | tf_op jit(solution)/shard_map/psum | solution.py:113
  46.2 274.9 %all-gather.6.cloned.1.call-start = ((), (), s32[]{:S(2)}) async-start(), calls=%async_computation.1 | async-start | bytes 47185920 | tf_op jit(solution)/shard_map/all_gather | solution.py:72
  58.9 0.9 copy-start.5
  59.0 11.7 %copy-start.8 = (u32[32]{0:T(128)S(1)}, u32[32]{0:T(128)}, u32[]{:S(2)}) copy-start(u32[32]{0:T(128)} %constant.34) | copy-start | bytes 388
  59.0 13.0 %copy-start.7 = (s32[16]{0:T(128)S(1)}, s32[16]{0:T(128)}, u32[]{:S(2)}) copy-start(s32[16]{0:T(128)} %param.23) | copy-start | bytes 196
  59.0 33.2 %copy-start.6 = (bf16[16,128]{1,0:T(8,128)(2,1)S(1)}, bf16[16,128]{1,0:T(8,128)(2,1)}, u32[]{:S(2)}) copy-start(bf16[16,128]{1,0:T(8,128)(2,1)} %param.18) | copy-start | bytes 12292
  59.0 430.6 %all-gather.4.cloned.1.call-start = ((), (), s32[]{:S(2)}) async-start(), calls=%async_computation | async-start | bytes 11796480 | tf_op jit(solution)/shard_map/all_gather | solution.py:85
  103.8 19.4 %copy-start.4 = (bf16[16,18432]{1,0:T(8,128)(2,1)S(1)}, bf16[16,18432]{1,0:T(8,128)(2,1)}, u32[]{:S(2)}) copy-start(bf16[16,18432]{1,0:T(8,128)(2,1)} %get-tuple-element.21) | copy-start | bytes 1769476
  127.8 9.7 %copy-start.2 = (bf16[16,32768]{1,0:T(8,128)(2,1)S(1)}, bf16[16,32768]{1,0:T(8,128)(2,1)}, u32[]{:S(2)}) copy-start(bf16[16,32768]{1,0:T(8,128)(2,1)} %get-tuple-element.20) | copy-start | bytes 3145732
  143.1 178.1 %copy-start.3 = (f32[144,2048]{1,0:T(8,128)S(1)}, f32[144,2048]{1,0:T(8,128)}, u32[]{:S(2)}) copy-start(f32[144,2048]{1,0:T(8,128)} %reshape.76) | copy-start | bytes 3538948
  489.6 27.9 %copy-start.1 = (bf16[512,2048]{1,0:T(8,128)(2,1)S(1)}, bf16[512,2048]{1,0:T(8,128)(2,1)}, u32[]{:S(2)}) copy-start(bf16[512,2048]{1,0:T(8,128)(2,1)} %param.12) | copy-start | bytes 6291460
Sparse Core Ops, SparseCore 0:
  46.3 45.8 all-reduce.4
  93.9 227.2 all-gather.5
  322.8 166.7 all-gather.3
where the time goes:
time: 525 us; the launch traced here: 524 us
  waiting for transfers between devices  325 us (62%)
  matrix products  62 us (12%)
  local copies, waits for them, and re-layouts  46.3 us (9%)
  blocking collectives  42.1 us (8%)
  other arithmetic  32.7 us (6%)
  between operations  16 us (3%)
    all_gather x1, waiting for transfers between devices, shards(): lax.all_gather(base_codes, 'dp', axis=1, tiled=True)  162 us
    all_gather x1, waiting for transfers between devices, shards(): lax.all_gather(masked, 'fsdp', axis=1, tiled=True)  142 us
    unnamed x22, local copies, waits for them, and re-layouts  42.4 us
    convert_element_type x1, other arithmetic, shards(): weight = (codes_all.astype(jnp.float32).reshape(width_part, block_count,...  26.4 us
    dot_general x1, matrix products, shards(): lax.dot_general(lax.all_gather(masked, 'fsdp', axis=1, tiled=True), weigh...  25.8 us
    psum x1, blocking collectives, shards(): lax.psum(outer_part.astype(jnp.bfloat16), 'fsdp').astype(jnp.float32)  20.8 us
    psum x1, waiting for transfers between devices, shards(): lax.psum(task_down.astype(jnp.bfloat16), 'dp').astype(jnp.float32)  20.1 us
    dot_general x1, matrix products, shards(): lax.dot_general(state_wide, sum_down, (((0,), (0,)), ((), ())), precision...  11.6 us
  transfers between devices with their start and end apart: 3, of which 3 were waited for; matrix products, arithmetic and copies ran while one was open for 18% of the time, Pallas kernels for 0%

commit v1 on v0

--- a/solution.py
+++ b/solution.py
@@ -9,6 +9,18 @@
 QBLOCK = 64
 SLOTS = 4
 adapter_scale = 2.0
+
+
+def gather_around(value, axis, dim):
+    ways, here, step = (lax.axis_size(axis), lax.axis_index(axis), value.shape[dim])
+    shape = [n * ways if d == dim else n for d, n in enumerate(value.shape)]
+    full = lax.dynamic_update_slice_in_dim(
+        jnp.zeros(shape, value.dtype), value, here * step, axis=dim
+    )
+    for far in range(1, ways):
+        value = lax.ppermute(value, axis, [(d, (d + 1) % ways) for d in range(ways)])
+        full = lax.dynamic_update_slice_in_dim(full, value, (here - far) % ways * step, axis=dim)
+    return full
 
 
 def shards(
@@ -82,7 +94,7 @@
         .astype(jnp.bfloat16)
     )
     merged_rows = lax.dot_general(
-        lax.all_gather(masked, "fsdp", axis=1, tiled=True),
+        gather_around(masked, "fsdp", 1),
         weight,
         (((1,), (1,)), ((), ())),
         preferred_element_type=jnp.float32,

time: 525 us -> 386 us (0.74)
  waiting for transfers between devices: 325 us -> 171 us
  local copies, waits for them, and re-layouts: 46.3 us -> 60.6 us
    all_gather x1 -> x0, waiting for transfers between devices: 142 us -> none  [shards(): lax.all_gather(masked, 'fsdp', axis=1, tiled=True)]
    ppermute x0 -> x3, waiting for transfers between devices: none -> 76.1 us  [gather_around(): lax.ppermute(value, axis, [(d, (d + 1) % ways) for d in range(ways)])]
    all_gather x1, waiting for transfers between devices: 162 us -> 95.2 us  [shards(): lax.all_gather(base_codes, 'dp', axis=1, tiled=True)]
    psum x1, waiting for transfers between devices: 20.1 us -> 0.01 us  [shards(): lax.psum(task_down.astype(jnp.bfloat16), 'dp').astype(jnp.float32)]
    dynamic_update_slice x0 -> x3, local copies, waits for them, and re-layouts: none -> 10 us  [gather_around(): lax.dynamic_update_slice_in_dim(full, value, (here - far) % ways * step,...]
    unnamed x22 -> x26, local copies, waits for them, and re-layouts: 42.4 us -> 41.8 us
  transfers between devices with their start and end apart: 3 -> 5, of which waited for: 3 -> 3; matrix products, arithmetic and copies ran while one was open for 18% -> 20% of each run, Pallas kernels for 0% -> 0%
where the time goes in v1:
time: 386 us; the launch traced here: 385 us
  waiting for transfers between devices  171 us (44%)
  matrix products  60.8 us (16%)
  local copies, waits for them, and re-layouts  60.6 us (16%)
  blocking collectives  44.8 us (12%)
  other arithmetic  30.7 us (8%)
  between operations  16.3 us (4%)
    all_gather x1, waiting for transfers between devices, shards(): lax.all_gather(base_codes, 'dp', axis=1, tiled=True)  95.2 us
    ppermute x3, waiting for transfers between devices, gather_around(): lax.ppermute(value, axis, [(d, (d + 1) % ways) for d in range(ways)])  76.1 us
    unnamed x26, local copies, waits for them, and re-layouts  41.8 us
    dot_general x1, matrix products, shards(): lax.dot_general(gather_around(masked, 'fsdp', 1), weight, (((1,), (1,)),...  27.8 us
    convert_element_type x1, other arithmetic, shards(): weight = (codes_all.astype(jnp.float32).reshape(width_part, block_count,...  25.7 us
    psum x1, blocking collectives, shards(): lax.psum(outer_part.astype(jnp.bfloat16), 'fsdp').astype(jnp.float32)  20.8 us
    unnamed x1, blocking collectives  12.2 us
    all_gather x1, blocking collectives, shards(): lax.all_gather(base_scales, 'dp', axis=1, tiled=True)  11.8 us
  transfers between devices with their start and end apart: 5, of which 3 were waited for; matrix products, arithmetic and copies ran while one was open for 20% of the time, Pallas kernels for 0%

profile of v1, /device:TPU:0, one launch (start us, length us, event | category | flops | bytes accessed | tf_op | source)
XLA Modules:
  0.0 384.8 jit_solution(6210998513418669568)
XLA Ops:
  7.2 0.0 copy-start
  7.2 0.0 all-reduce.5.cloned.1.call-start
  8.7 1.3 fusion.16
  10.0 1.5 fusion.14
  11.5 0.4 reshape.73
  11.9 0.7 reshape.72
  12.6 0.2 copy.34
  12.8 0.0 copy-done
  12.8 0.7 fusion.2
  13.5 0.0 copy-start.6
  13.5 4.8 %broadcast_in_dim.27 = bf16[512,9216]{1,0:T(8,128)(2,1)} broadcast(bf16[]{:T(256)} %constant.47.clone.1), dimensions={} | broadcast | bytes 9437186 | tf_op jit(solution)/shard_map/broadcast_in_dim | solution.py:18
  18.3 0.0 copy-done.6
  18.3 2.0 constant_dynamic-update-slice_fusion.3
  20.3 0.0 copy-start.2
  20.3 1.4 copy-done.2
  21.7 0.7 convolution_convert_fusion.1
  22.4 20.8 %all-reduce.2 = (bf16[512,16]{0,1:T(8,128)(2,1)S(1)}, bf16[512,16]{0,1:T(8,128)(2,1)S(1)}) all-reduce(bf16[512,16]{0,1:T(8,128)(2,1)S(1)} %convolution_convert_fusion.1, bf16[512,16]{0,1:T(8,128)(2,1)S(1)} %fusion.2), channel_id=1, replica_groups=mesh['groups'=2,'fsdp'=4,'dp'=4] {'fsdp'}, use_global_device_ids=true, to_apply=%region_0.1 | all-reduce | flops 16384 | bytes 65536 | tf_op jit(solution)/shard_map/psum | solution.py:79
  43.3 2.1 fusion.23
  45.4 0.4 fusion.1
  45.8 0.3 copy.36
  46.1 0.3 mul.101
  46.4 0.4 copy.37
  46.8 0.6 mul.107
  47.4 1.2 multiply_convert_fusion
  48.5 1.0 multiply_convert_fusion.1
  49.5 0.0 all-reduce.5.cloned.1.call-update
  49.5 0.0 all-gather.3.cloned.1.call-start
  49.5 12.6 %copy.33 = bf16[2048,2304]{0,1:T(8,128)(2,1)} copy(bf16[2048,2304]{1,0:T(8,128)(2,1)} %param.14) | data formatting | bytes 18874368 | tf_op args[2]
  62.2 0.0 all-gather.3.cloned.1.call-update
  62.2 0.0 copy-start.8
  62.2 0.1 collective-permute-start
  62.3 51.4 %collective-permute-done = bf16[512,2304]{1,0:T(8,128)(2,1)} collective-permute-done((bf16[512,2304]{1,0:T(8,128)(2,1)}, bf16[512,2304]{1,0:T(8,128)(2,1)}, u32[]{:S(2)}, u32[]{:S(2)}) %collective-permute-start) | collective-permute-done | bytes 2359328 | tf_op jit(solution)/shard_map/ppermute | solution.py:21
  113.7 0.0 collective-permute-start.1
  113.7 0.0 copy-done.7
  113.7 11.8 %all-gather = bf16[4,36,2048]{2,1,0:T(8,128)(2,1)S(1)} all-gather(bf16[1,36,2048]{2,1,0:T(8,128)(2,1)S(1)} %bitcast.56), channel_id=1, replica_groups=mesh['groups'=2,'fsdp'=4,'dp'=4] {'dp'}, dimensions={0}, use_global_device_ids=true | all-gather | bytes 737280 | tf_op jit(solution)/shard_map/all_gather | solution.py:85
  125.5 1.1 reshape.76
  126.6 0.0 copy-done.10
  126.7 0.6 dynamic-slice
  127.9 0.0 copy-done.9
  127.9 0.2 convert_reduce_fusion
  128.1 2.8 fusion.21
  130.9 0.0 copy-done.8
  130.9 9.5 %convolution_bitcast_fusion = f32[128,32768]{0,1:T(8,128)} fusion(bf16[16,32768]{1,0:T(8,128)(2,1)} %get-tuple-element.20, bf16[16,128]{1,0:T(8,128)(2,1)S(1)} %copy-done.8), kind=kOutput, calls=%fused_computation.2 | convolution fusion | flops 134217728 | bytes 17829888 | tf_op jit(solution)/shard_map/dot_general | solution.py:129
  140.4 24.7 %collective-permute-done.1 = bf16[512,2304]{1,0:T(8,128)(2,1)} collective-permute-done((bf16[512,2304]{1,0:T(8,128)(2,1)}, bf16[512,2304]{1,0:T(8,128)(2,1)}, u32[]{:S(2)}, u32[]{:S(2)}) %collective-permute-start.1) | collective-permute-done | bytes 2359328 | tf_op jit(solution)/shard_map/ppermute | solution.py:21
  165.1 0.0 collective-permute-start.2
  165.1 0.0 copy-done.5
  165.1 4.6 %convolution_bitcast_fusion.1 = f32[128,18432]{0,1:T(8,128)} fusion(bf16[16,18432]{1,0:T(8,128)(2,1)S(1)} %copy-done.5, bf16[16,128]{1,0:T(8,128)(2,1)S(1)} %copy-done.8), kind=kOutput, calls=%fused_computation.3 | convolution fusion | flops 75497472 | bytes 10031104 | tf_op jit(solution)/shard_map/dot_general | solution.py:130
  169.7 9.6 %copy.39 = f32[128,18432]{1,0:T(8,128)} copy(f32[128,18432]{0,1:T(8,128)} %convolution_bitcast_fusion.1) | data formatting | bytes 18874368
  179.3 17.5 %copy.38 = f32[128,32768]{1,0:T(8,128)} copy(f32[128,32768]{0,1:T(8,128)} %convolution_bitcast_fusion) | data formatting | bytes 33554432
  196.8 0.0 copy-done.3
  196.9 5.7 %fusion.22 = f32[16,128]{1,0:T(8,128)S(1)} fusion(bf16[16,32768]{1,0:T(8,128)(2,1)S(1)} %copy-done.3, bf16[128,32768]{1,0:T(8,128)(2,1)} %param.19), kind=kOutput, calls=%fused_computation.51 | convolution fusion | flops 134217728 | bytes 9445376 | tf_op jit(solution)/shard_map/dot_general | solution.py:131
  202.6 3.7 convolution_add_fusion
  206.3 0.1 convolution_convert_fusion.2
  206.4 12.2 %all-reduce = bf16[16,128]{1,0:T(8,128)(2,1)S(1)} all-reduce(bf16[16,128]{1,0:T(8,128)(2,1)S(1)} %convolution_convert_fusion.2), channel_id=2, replica_groups=mesh['groups'=2,'fsdp'=4,'dp'=4] {'fsdp'}, use_global_device_ids=true, to_apply=%region_5.6.clone | all-reduce | flops 2048 | bytes 8192
  218.6 0.6 dynamic-slice_convert_fusion
  219.2 3.3 constant_dynamic-update-slice_fusion.2
  222.5 3.4 constant_dynamic-update-slice_fusion.1
  225.9 0.0 collective-permute-done.2
  225.9 3.4 constant_dynamic-update-slice_fusion
  229.2 95.2 %all-gather.3.cloned.1.call-done = bf16[2048,9216]{0,1:T(8,128)(2,1)} async-done(((bf16[2048,2304]{0,1:T(8,128)(2,1)}), bf16[2048,9216]{0,1:T(8,128)(2,1)}) %all-gather.3.cloned.1.call-update) | async-done | bytes 37748752 | tf_op jit(solution)/shard_map/all_gather | solution.py:84
  324.5 0.0 copy-done.4
  324.5 25.7 %fusion = bf16[2048,9216]{0,1:T(8,128)(2,1)} fusion(bf16[2048,9216]{0,1:T(8,128)(2,1)} %all-gather.3.cloned.1.call-done, f32[2048,144]{0,1:T(8,128)S(1)} %bitcast.53), kind=kLoop, calls=%fused_computation.1 | loop fusion | flops 56623104 | bytes 76677120 | tf_op jit(solution)/shard_map/convert_element_type | solution.py:94
  350.2 27.8 %add_convert_fusion = bf16[512,2048]{1,0:T(8,128)(2,1)} fusion(f32[512,2048]{1,0:T(8,128)} %fusion.21, bf16[512,9216]{1,0:T(8,128)(2,1)} %constant_dynamic-update-slice_fusion, bf16[2048,9216]{0,1:T(8,128)(2,1)} %fusion), kind=kOutput, calls=%fused_computation.4 | convolution fusion | flops 19330498560 | bytes 53477376 | tf_op jit(solution)/shard_map/dot_general | solution.py:96
  378.0 0.0 copy-done.1
  (16 shorter events, 0.1 us)
Async XLA Ops:
  7.2 5.6 %copy-start = (bf16[512,2048]{1,0:T(8,128)(2,1)S(1)}, bf16[512,2048]{1,0:T(8,128)(2,1)}, u32[]{:S(2)}) copy-start(bf16[512,2048]{1,0:T(8,128)(2,1)} %param.12) | copy-start | bytes 6291460
  7.2 123.7 %all-reduce.5.cloned.1.call-start = ((), (), s32[]{:S(2)}) async-start(), calls=%async_computation.1 | async-start | bytes 3276800 | tf_op jit(solution)/shard_map/psum | solution.py:125
  13.5 4.8 %copy-start.6 = (bf16[512,2304]{1,0:T(8,128)(2,1)S(1)}, bf16[512,2304]{1,0:T(8,128)(2,1)}, u32[]{:S(2)}) copy-start(bf16[512,2304]{1,0:T(8,128)(2,1)} %param.13) | copy-start | bytes 7077892
  20.3 1.4 copy-start.2
  49.5 275.0 %all-gather.3.cloned.1.call-start = ((), (), s32[]{:S(2)}) async-start(), calls=%async_computation | async-start | bytes 47185920 | tf_op jit(solution)/shard_map/all_gather | solution.py:84
  62.2 51.5 %copy-start.7 = (bf16[2048,36]{0,1:T(8,128)(2,1)S(1)}, bf16[2048,36]{0,1:T(8,128)(2,1)}, u32[]{:S(2)}) copy-start(bf16[2048,36]{0,1:T(8,128)(2,1)} %param.15) | copy-start | bytes 442372
  62.2 64.5 %copy-start.10 = (u32[32]{0:T(128)S(1)}, u32[32]{0:T(128)}, u32[]{:S(2)}) copy-start(u32[32]{0:T(128)} %constant.65) | copy-start | bytes 388
  62.2 65.7 %copy-start.9 = (s32[16]{0:T(128)S(1)}, s32[16]{0:T(128)}, u32[]{:S(2)}) copy-start(s32[16]{0:T(128)} %param.23) | copy-start | bytes 196
  62.2 68.6 %copy-start.8 = (bf16[16,128]{1,0:T(8,128)(2,1)S(1)}, bf16[16,128]{1,0:T(8,128)(2,1)}, u32[]{:S(2)}) copy-start(bf16[16,128]{1,0:T(8,128)(2,1)} %param.18) | copy-start | bytes 12292
  62.2 51.5 %collective-permute-start = (bf16[512,2304]{1,0:T(8,128)(2,1)}, bf16[512,2304]{1,0:T(8,128)(2,1)}, u32[]{:S(2)}, u32[]{:S(2)}) collective-permute-start(bf16[512,2304]{1,0:T(8,128)(2,1)} %copy-done.2), channel_id=1, source_target_pairs={{0,4},{4,8},{8,12},{12,0},{1,5},{5,9},{9,13},{13,1},{2,6},{6,10},{... | collective-permute-start | bytes 7077896 | tf_op jit(solution)/shard_map/ppermute | solution.py:21
  113.7 51.4 %collective-permute-start.1 = (bf16[512,2304]{1,0:T(8,128)(2,1)}, bf16[512,2304]{1,0:T(8,128)(2,1)}, u32[]{:S(2)}, u32[]{:S(2)}) collective-permute-start(bf16[512,2304]{1,0:T(8,128)(2,1)} %collective-permute-done), channel_id=1, source_target_pairs={{0,4},{4,8},{8,12},{12,0},{1,5},{5,9},{9,13},{13,1},{2,6},{6,10},{... | collective-permute-start | bytes 7077896 | tf_op jit(solution)/shard_map/ppermute | solution.py:21
  130.9 34.2 %copy-start.5 = (bf16[16,18432]{1,0:T(8,128)(2,1)S(1)}, bf16[16,18432]{1,0:T(8,128)(2,1)}, u32[]{:S(2)}) copy-start(bf16[16,18432]{1,0:T(8,128)(2,1)} %get-tuple-element.21) | copy-start | bytes 1769476
  165.1 60.7 %collective-permute-start.2 = (bf16[512,2304]{1,0:T(8,128)(2,1)}, bf16[512,2304]{1,0:T(8,128)(2,1)}, u32[]{:S(2)}, u32[]{:S(2)}) collective-permute-start(bf16[512,2304]{1,0:T(8,128)(2,1)} %collective-permute-done.1), channel_id=1, source_target_pairs={{0,4},{4,8},{8,12},{12,0},{1,5},{5,9},{9,13},{13,1},{2,6},{6,10},{... | collective-permute-start | bytes 7077896 | tf_op jit(solution)/shard_map/ppermute | solution.py:21
  179.3 17.5 %copy-start.3 = (bf16[16,32768]{1,0:T(8,128)(2,1)S(1)}, bf16[16,32768]{1,0:T(8,128)(2,1)}, u32[]{:S(2)}) copy-start(bf16[16,32768]{1,0:T(8,128)(2,1)} %get-tuple-element.20) | copy-start | bytes 3145732
  222.5 102.0 %copy-start.4 = (f32[144,2048]{1,0:T(8,128)S(1)}, f32[144,2048]{1,0:T(8,128)}, u32[]{:S(2)}) copy-start(f32[144,2048]{1,0:T(8,128)} %reshape.76) | copy-start | bytes 3538948
  350.2 27.8 %copy-start.1 = (bf16[512,2048]{1,0:T(8,128)(2,1)S(1)}, bf16[512,2048]{1,0:T(8,128)(2,1)}, u32[]{:S(2)}) copy-start(bf16[512,2048]{1,0:T(8,128)(2,1)} %param.12) | copy-start | bytes 6291460
Sparse Core Ops, SparseCore 0:
  49.6 42.3 all-reduce.4
  93.7 230.7 all-gather.2
